TPU v7x, 256 devices: a whole 4x4x8 slice. The times are simulated.
256 devices in a mesh: tok: 16 (over y, x), col: 16 (over z, core).
Axes of the slice: x: 4, y: 4, z: 8, core: 2. Of those that a mesh axis runs over, the one named last changes fastest.
Arguments:
- activations: bfloat16 [32768, 8192], P('tok', 'col'), may hold values from -60 to 60, as said below
- weight: bfloat16 [8192, 8192], P('tok', 'col'), may hold values from -6 to 6
- keep_mask: int32 [8192, 8192], P('tok', 'col'), may hold values from 0 to 1
Outputs:
- new_weight: bfloat16 [8192, 8192], P('tok', 'col')
Inputs may be any that keep to these rules, and one draw needn't show every extreme that they name: activations of calibration tokens.
All inputs are finite; a program needn't handle non-finite values.
Results may differ from a plain program's by a relative error of at most 0.00115.
Values may be sent and summed in bfloat16 or wider, within the bound.
A program may use at most 64 MiB of HBM per device.

v0:
```python
import jax
import jax.numpy as jnp
from jax import lax
from jax.sharding import PartitionSpec as P

B = 1024
ITERS = 4


def per_device(activations, weight, keep_mask):
    highest = lax.Precision.HIGHEST
    n_col = lax.axis_size("col")
    n_tok = lax.axis_size("tok")
    tok_rows = activations.shape[0]
    panel_width = B // n_col
    total_count = tok_rows * n_tok
    partial_panel = lax.dot_general(
        activations,
        lax.all_gather(activations[:, :panel_width], "col", axis=1, tiled=True),
        (((0,), (0,)), ((), ())),
        preferred_element_type=jnp.float32,
    )
    hessian_panel = lax.psum(partial_panel, "tok") / total_count
    block_part = hessian_panel[:panel_width]
    diagonal_block = lax.all_gather(block_part, "col", axis=0, tiled=True)
    identity = jnp.eye(B, dtype=jnp.float32)
    damping = 0.01 * jnp.mean(jnp.diagonal(diagonal_block))
    damped = diagonal_block + damping * identity
    frobenius = jnp.sqrt(jnp.sum(damped * damped))
    col_index = lax.axis_index("col")
    row_ids = col_index * panel_width + lax.iota(jnp.int32, panel_width)
    iterate = (row_ids[:, None] == lax.iota(jnp.int32, B)[None, :]).astype(jnp.float32) / frobenius
    for sweep in range(ITERS):
        if sweep == 0:
            whole = identity / frobenius
        else:
            whole = lax.all_gather(iterate.astype(jnp.bfloat16), "col", axis=0, tiled=True).astype(
                iterate.dtype
            )
        product = jnp.dot(iterate, damped, precision=highest)
        iterate = 2.0 * iterate - jnp.dot(product, whole, precision=highest)
    inverse = lax.all_gather(iterate, "col", axis=0, tiled=True)
    pruned = jnp.where(
        keep_mask[:, :panel_width] == 0, weight[:, :panel_width], jnp.zeros((), jnp.bfloat16)
    )
    pruned_panel = lax.all_gather(pruned, "col", axis=1, tiled=True).astype(jnp.float32)
    factor_rows = jnp.dot(pruned_panel, inverse, precision=highest)
    correction = lax.dot_general(
        factor_rows, hessian_panel, (((1,), (1,)), ((), ())), precision=highest
    )
    kept = keep_mask.astype(jnp.float32)
    return (kept * (weight.astype(jnp.float32) - correction)).astype(jnp.bfloat16)


def solution(mesh):
    return jax.shard_map(
        per_device,
        mesh=mesh,
        in_specs=(P("tok", "col"), P("tok", "col"), P("tok", "col")),
        out_specs=P("tok", "col"),
        check_vma=False,
    )
```

profile of v0, /device:TPU:1, one launch (start us, length us, event | category | flops | bytes accessed | tf_op | source)
XLA Modules:
  0.0 456.3 jit_solution(11155648659330884020)
XLA Ops:
  6.5 1.1 slice.14
  7.6 0.9 copy.9
  8.5 0.0 all-gather.10.cloned.1.call-update
  8.5 0.0 all-reduce.2.cloned.1.call-start
  8.6 47.0 %all-gather.10.cloned.1.call-done = bf16[2048,1024]{0,1:T(8,128)(2,1)} async-done(((bf16[2048,64]{0,1:T(8,128)(2,1)}), bf16[2048,1024]{0,1:T(8,128)(2,1)}) %all-gather.10.cloned.1.call-update) | async-done | bytes 4194320 | tf_op jit(solution)/shard_map/all_gather | solution.py:19
  55.5 6.6 %fusion.25 = f32[512,1024]{1,0:T(8,128)} fusion(bf16[2048,512]{1,0:T(8,128)(2,1)} %param.3, bf16[2048,1024]{0,1:T(8,128)(2,1)} %all-gather.10.cloned.1.call-done), kind=kOutput, calls=%fused_computation.37 | convolution fusion | flops 2147483648 | bytes 8388608 | tf_op jit(solution)/shard_map/dot_general | solution.py:17
  62.1 0.0 all-reduce.2.cloned.1.call-update
  62.2 0.0 all-gather.12.cloned.1.call-start
  62.2 97.5 %all-reduce.2.cloned.1.call-done = f32[512,1024]{1,0:T(8,128)} async-done(((f32[512,1024]{1,0:T(8,128)}), f32[512,1024]{1,0:T(8,128)}) %all-reduce.2.cloned.1.call-update) | async-done | bytes 2097168 | tf_op jit(solution)/shard_map/psum | solution.py:23
  159.7 1.8 broadcast_multiply_fusion
  161.5 0.7 slice.18
  162.2 0.0 all-gather.12.cloned.1.call-update
  162.3 0.0 all-gather.14.cloned.1.call-start
  162.3 43.1 %all-gather.12.cloned.1.call-done = f32[1024,1024]{1,0:T(8,128)} async-done(((f32[64,1024]{1,0:T(8,128)}), f32[1024,1024]{1,0:T(8,128)}) %all-gather.12.cloned.1.call-update) | async-done | bytes 4194320 | tf_op jit(solution)/shard_map/all_gather | solution.py:25
  205.5 17.2 %gather_fusion = f32[1024]{0:T(1024)S(1)} fusion(f32[1024,1024]{1,0:T(8,128)} %all-gather.12.cloned.1.call-done, s32[1024]{0:T(1024)S(1)} %bitcast.16), kind=kCustom, calls=%fused_computation | custom fusion | bytes 16384 | tf_op jit(solution)/shard_map/jit(diagonal)/cond/branch_0_fun/gather | solution.py:27
  222.7 0.6 reduce_sum.18
  223.9 3.9 multiply_reduce_fusion
  228.5 4.9 %fusion.9 = f32[64,1024]{1,0:T(8,128)S(1)} fusion(f32[1024,1024]{1,0:T(8,128)} %all-gather.12.cloned.1.call-done, f32[]{:T(128)S(6)} %mul_shard_map.3, f32[]{:T(128)S(6)} %sqrt.3, s32[64]{0:T(128)S(1)} %iota_add_fusion), kind=kOutput, calls=%fused_computation.14 | convolution fusion | flops 808583168 | bytes 4456712 | tf_op jit(solution)/shard_map/dot_general | solution.py:40
  233.4 1.9 fusion.22
  235.3 0.0 all-gather.14.cloned.1.call-update
  235.3 0.0 all-gather.16.cloned.1.call-start
  235.4 4.9 %fusion.8 = f32[64,1024]{1,0:T(8,128)S(1)} fusion(f32[64,1024]{1,0:T(8,128)S(1)} %get-tuple-element.6, f32[1024,1024]{1,0:T(8,128)} %all-gather.12.cloned.1.call-done, f32[]{:T(128)S(6)} %mul_shard_map.3), kind=kOutput, calls=%fused_computation.13 | convolution fusion | flops 808452096 | bytes 4718596 | tf_op jit(solution)/shard_map/dot_general | solution.py:40
  240.3 33.5 %all-gather.14.cloned.1.call-done = bf16[1024,1024]{1,0:T(8,128)(2,1)} async-done(((bf16[64,1024]{1,0:T(8,128)(2,1)}), bf16[1024,1024]{1,0:T(8,128)(2,1)}) %all-gather.14.cloned.1.call-update) | async-done | bytes 2097168 | tf_op jit(solution)/shard_map/all_gather | solution.py:37
  273.8 3.5 fusion.23
  277.3 0.0 all-gather.16.cloned.1.call-update
  277.3 0.2 all-gather.18.cloned.1.call-start
  277.5 0.0 slice-start
  277.5 0.0 slice-start.1
  277.5 4.9 %fusion.7 = f32[64,1024]{1,0:T(8,128)S(1)} fusion(f32[64,1024]{1,0:T(8,128)S(1)} %get-tuple-element.8, f32[1024,1024]{1,0:T(8,128)} %all-gather.12.cloned.1.call-done, f32[]{:T(128)S(6)} %mul_shard_map.3), kind=kOutput, calls=%fused_computation.12 | convolution fusion | flops 808452096 | bytes 4718596 | tf_op jit(solution)/shard_map/dot_general | solution.py:40
  282.5 33.0 %all-gather.16.cloned.1.call-done = bf16[1024,1024]{1,0:T(8,128)(2,1)} async-done(((bf16[64,1024]{1,0:T(8,128)(2,1)}), bf16[1024,1024]{1,0:T(8,128)(2,1)}) %all-gather.16.cloned.1.call-update) | async-done | bytes 2097168 | tf_op jit(solution)/shard_map/all_gather | solution.py:37
  315.5 3.5 fusion.24
  318.9 0.0 all-gather.18.cloned.1.call-update
  319.0 0.0 all-gather.8.cloned.1.call-start
  319.0 0.1 copy.7
  319.1 0.1 copy.8
  319.3 0.6 compare_select_fusion
  319.9 0.0 all-gather.8.cloned.1.call-update
  319.9 0.0 all-gather.20.cloned.1.call-start
  320.0 4.9 %fusion.6 = f32[64,1024]{1,0:T(8,128)S(1)} fusion(f32[64,1024]{1,0:T(8,128)S(1)} %get-tuple-element.10, f32[1024,1024]{1,0:T(8,128)} %all-gather.12.cloned.1.call-done, f32[]{:T(128)S(6)} %mul_shard_map.3), kind=kOutput, calls=%fused_computation.11 | convolution fusion | flops 808452096 | bytes 4718596 | tf_op jit(solution)/shard_map/dot_general | solution.py:40
  324.9 32.3 %all-gather.18.cloned.1.call-done = bf16[1024,1024]{1,0:T(8,128)(2,1)} async-done(((bf16[64,1024]{1,0:T(8,128)(2,1)}), bf16[1024,1024]{1,0:T(8,128)(2,1)}) %all-gather.18.cloned.1.call-update) | async-done | bytes 2097168 | tf_op jit(solution)/shard_map/all_gather | solution.py:37
  357.2 3.5 convolution_subtract_fusion.1
  360.7 0.0 all-gather.20.cloned.1.call-update
  360.7 35.4 %all-gather.8.cloned.1.call-done = bf16[512,1024]{0,1:T(8,128)(2,1)} async-done(((bf16[512,64]{0,1:T(8,128)(2,1)}), bf16[512,1024]{0,1:T(8,128)(2,1)}) %all-gather.8.cloned.1.call-update) | async-done | bytes 1048592 | tf_op jit(solution)/shard_map/all_gather | solution.py:46
  396.1 42.8 %all-gather.20.cloned.1.call-done = f32[1024,1024]{1,0:T(8,128)} async-done(((f32[64,1024]{1,0:T(8,128)}), f32[1024,1024]{1,0:T(8,128)}) %all-gather.20.cloned.1.call-update) | async-done | bytes 4194320 | tf_op jit(solution)/shard_map/all_gather | solution.py:42
  438.9 6.1 %fusion.26 = f32[512,1024]{1,0:T(8,128)S(1)} fusion(bf16[512,1024]{0,1:T(8,128)(2,1)} %all-gather.8.cloned.1.call-done, f32[1024,1024]{1,0:T(8,128)} %all-gather.20.cloned.1.call-done), kind=kOutput, calls=%fused_computation.38 | convolution fusion | flops 6442450944 | bytes 7340032 | tf_op jit(solution)/shard_map/dot_general | solution.py:47
  445.0 0.0 copy-done
  445.0 0.0 copy-done.1
  445.0 4.5 fusion.5
  (9 shorter events, 0.0 us)
Async XLA Ops:
  6.5 49.0 %all-gather.10.cloned.1.call-start = ((), (), s32[]{:S(2)}) async-start(), calls=%async_computation.1 | async-start | bytes 4456448 | tf_op jit(solution)/shard_map/all_gather | solution.py:19
  8.5 151.2 %all-reduce.2.cloned.1.call-start = ((), (), s32[]{:S(2)}) async-start(), calls=%async_computation.2 | async-start | bytes 4194304 | tf_op jit(solution)/shard_map/psum | solution.py:23
  62.2 143.3 %all-gather.12.cloned.1.call-start = ((), (), s32[]{:S(2)}) async-start(), calls=%async_computation.3 | async-start | bytes 4456448 | tf_op jit(solution)/shard_map/all_gather | solution.py:25
  162.3 111.5 %all-gather.14.cloned.1.call-start = ((), (), s32[]{:S(2)}) async-start(), calls=%async_computation.4 | async-start | bytes 2228224 | tf_op jit(solution)/shard_map/all_gather | solution.py:37
  235.3 80.1 %all-gather.16.cloned.1.call-start = ((), (), s32[]{:S(2)}) async-start(), calls=%async_computation.5 | async-start | bytes 2228224 | tf_op jit(solution)/shard_map/all_gather | solution.py:37
  277.3 79.9 %all-gather.18.cloned.1.call-start = ((), (), s32[]{:S(2)}) async-start(), calls=%async_computation.6 | async-start | bytes 2228224 | tf_op jit(solution)/shard_map/all_gather | solution.py:37
  277.5 41.5 %slice-start = ((s32[512,512]{1,0:T(8,128)}), s32[512,64]{1,0:T(8,128)S(1)}, s32[]{:S(2)}) async-start(s32[512,512]{1,0:T(8,128)} %param.5), calls=%async_computation.8 | async-start | bytes 524288 | tf_op jit(solution)/shard_map/slice | solution.py:44
  277.5 41.6 %slice-start.1 = ((bf16[512,512]{1,0:T(8,128)(2,1)}), bf16[512,64]{1,0:T(8,128)(2,1)S(1)}, s32[]{:S(2)}) async-start(bf16[512,512]{1,0:T(8,128)(2,1)} %param.4), calls=%async_computation.9 | async-start | bytes 262144 | tf_op jit(solution)/shard_map/slice | solution.py:44
  319.0 77.2 %all-gather.8.cloned.1.call-start = ((), (), s32[]{:S(2)}) async-start(), calls=%async_computation | async-start | bytes 1114112 | tf_op jit(solution)/shard_map/all_gather | solution.py:46
  319.9 119.0 %all-gather.20.cloned.1.call-start = ((), (), s32[]{:S(2)}) async-start(), calls=%async_computation.7 | async-start | bytes 4456448 | tf_op jit(solution)/shard_map/all_gather | solution.py:42
  360.7 84.3 %copy-start = (f32[512,1024]{1,0:T(8,128)S(1)}, f32[512,1024]{1,0:T(8,128)}, u32[]{:S(2)}) copy-start(f32[512,1024]{1,0:T(8,128)} %all-reduce.2.cloned.1.call-done) | copy-start | bytes 6291460
  360.7 84.3 %copy-start.1 = (s32[512,512]{1,0:T(8,128)S(1)}, s32[512,512]{1,0:T(8,128)}, u32[]{:S(2)}) copy-start(s32[512,512]{1,0:T(8,128)} %param.5) | copy-start | bytes 3145732
  438.9 6.1 %copy-start.2 = (bf16[512,512]{1,0:T(8,128)(2,1)S(1)}, bf16[512,512]{1,0:T(8,128)(2,1)}, u32[]{:S(2)}) copy-start(bf16[512,512]{1,0:T(8,128)(2,1)} %param.4) | copy-start | bytes 1572868
Sparse Core Ops, SparseCore 0:
  9.2 46.3 all-gather.9
  62.3 97.4 all-reduce.1
  162.4 43.0 all-gather.11
  235.5 38.2 all-gather.13
  277.4 38.0 all-gather.15
  319.1 38.0 all-gather.17
  359.1 36.9 all-gather.7
  398.1 40.7 all-gather.19
where the time goes:
time: 457 us; the launch traced here: 456 us
  waiting for transfers between devices  365 us (80%)
  matrix products  49.1 us (11%)
  local copies, waits for them, and re-layouts  20.1 us (4%)
  between operations  15 us (3%)
  other arithmetic  6.89 us (2%)
    all_gather x3, waiting for transfers between devices, per_device(): lax.all_gather(iterate.astype(jnp.bfloat16), 'col', axis=0, tiled=True)  98.8 us
    psum x1, waiting for transfers between devices, per_device(): hessian_panel = lax.psum(partial_panel, 'tok') / total_count  97.5 us
    all_gather x1, waiting for transfers between devices, per_device(): lax.all_gather(activations[:, :panel_width], 'col', axis=1, tiled=True)  47 us
    all_gather x1, waiting for transfers between devices, per_device(): diagonal_block = lax.all_gather(block_part, 'col', axis=0, tiled=True)  43.1 us
    all_gather x1, waiting for transfers between devices, per_device(): inverse = lax.all_gather(iterate, 'col', axis=0, tiled=True)  42.8 us
    all_gather x1, waiting for transfers between devices, per_device(): lax.all_gather(pruned, 'col', axis=1, tiled=True).astype(jnp.float32)  35.4 us
    dot_general x4, matrix products, per_device(): product = jnp.dot(iterate, damped, precision=highest)  19.6 us
    gather x1, local copies, waits for them, and re-layouts, per_device(): damping = 0.01 * jnp.mean(jnp.diagonal(diagonal_block))  17.2 us
  transfers between devices with their start and end apart: 8, of which 8 were waited for; matrix products, arithmetic and copies ran while one was open for 4% of the time, Pallas kernels for 0%

commit v1 on v0

--- a/solution.py
+++ b/solution.py
@@ -1,3 +1,4 @@
+import functools
 import jax
 import jax.numpy as jnp
 from jax import lax
@@ -5,6 +6,17 @@
 
 B = 1024
 ITERS = 4
+
+
+def _save_islands(content, link_axis, dim_at):
+    new = tuple((content for _ in range(lax.psum(1, link_axis))))
+    a_now = jnp.stack(new, axis=0)
+    kept_arr = lax.all_to_all(a_now, link_axis, 0, 0)
+    outer = jnp.concatenate(kept_arr, dim_at)
+    return outer
+
+
+_solve_units = functools.partial(_save_islands, link_axis="col", dim_at=1)
 
 
 def per_device(activations, weight, keep_mask):
@@ -16,7 +28,7 @@
     total_count = tok_rows * n_tok
     partial_panel = lax.dot_general(
         activations,
-        lax.all_gather(activations[:, :panel_width], "col", axis=1, tiled=True),
+        _solve_units(activations[:, :panel_width]),
         (((0,), (0,)), ((), ())),
         preferred_element_type=jnp.float32,
     )

time: 457 us -> 512 us (1.12)
  blocking collectives: 0 us -> 106 us
  waiting for transfers between devices: 365 us -> 316 us
    all_to_all x0 -> x1, blocking collectives: none -> 106 us  [_save_islands(): kept_arr = lax.all_to_all(a_now, link_axis, 0, 0)]
    all_gather x1 -> x0, waiting for transfers between devices: 47 us -> none  [per_device(): lax.all_gather(activations[:, :panel_width], 'col', axis=1, tiled=True)]
  transfers between devices with their start and end apart: 8 -> 7, of which waited for: 8 -> 7; matrix products, arithmetic and copies ran while one was open for 4% -> 4% of each run, Pallas kernels for 0% -> 0%
where the time goes in v1:
time: 512 us; the launch traced here: 511 us
  waiting for transfers between devices  316 us (62%)
  blocking collectives  106 us (21%)
  matrix products  46.2 us (9%)
  local copies, waits for them, and re-layouts  20 us (4%)
  between operations  15 us (3%)
  other arithmetic  6.89 us (1%)
    all_to_all x1, blocking collectives, _save_islands(): kept_arr = lax.all_to_all(a_now, link_axis, 0, 0)  106 us
    all_gather x3, waiting for transfers between devices, per_device(): lax.all_gather(iterate.astype(jnp.bfloat16), 'col', axis=0, tiled=True)  98.8 us
    psum x1, waiting for transfers between devices, per_device(): hessian_panel = lax.psum(partial_panel, 'tok') / total_count  96.1 us
    all_gather x1, waiting for transfers between devices, per_device(): diagonal_block = lax.all_gather(block_part, 'col', axis=0, tiled=True)  43.1 us
    all_gather x1, waiting for transfers between devices, per_device(): inverse = lax.all_gather(iterate, 'col', axis=0, tiled=True)  42.8 us
    all_gather x1, waiting for transfers between devices, per_device(): lax.all_gather(pruned, 'col', axis=1, tiled=True).astype(jnp.float32)  35.2 us
    dot_general x4, matrix products, per_device(): product = jnp.dot(iterate, damped, precision=highest)  19.6 us
    gather x1, local copies, waits for them, and re-layouts, per_device(): damping = 0.01 * jnp.mean(jnp.diagonal(diagonal_block))  17.3 us
  transfers between devices with their start and end apart: 7, of which 7 were waited for; matrix products, arithmetic and copies ran while one was open for 4% of the time, Pallas kernels for 0%

profile of v1, /device:TPU:1, one launch (start us, length us, event | category | flops | bytes accessed | tf_op | source)
XLA Modules:
  0.0 510.5 jit_solution(8288772577103414900)
XLA Ops:
  6.5 0.0 all-reduce.2.cloned.1.call-start
  6.5 1.1 slice.14
  7.6 0.2 copy.7
  7.8 0.5 stack.2
  8.3 0.0 copy-start.3
  8.3 105.9 %all_to_all.5 = bf16[16,2048,64]{1,2,0:T(8,128)(2,1)S(1)} all-to-all(bf16[16,2048,64]{1,2,0:T(8,128)(2,1)S(1)} %stack.2), channel_id=1, replica_groups=mesh['tok'=16,'col'=16] {'col'}, dimensions={0} | all-to-all | bytes 8388608 | tf_op jit(solution)/shard_map/all_to_all | solution.py:14
  114.2 0.0 copy-done.3
  114.2 3.7 fusion.25
  117.9 0.0 all-reduce.2.cloned.1.call-update
  118.0 0.0 all-gather.9.cloned.1.call-start
  118.0 96.1 %all-reduce.2.cloned.1.call-done = f32[512,1024]{1,0:T(8,128)} async-done(((f32[512,1024]{1,0:T(8,128)}), f32[512,1024]{1,0:T(8,128)}) %all-reduce.2.cloned.1.call-update) | async-done | bytes 2097168 | tf_op jit(solution)/shard_map/psum | solution.py:35
  214.1 1.8 broadcast_multiply_fusion
  215.9 0.7 slice.18
  216.6 0.0 all-gather.9.cloned.1.call-update
  216.6 0.0 all-gather.11.cloned.1.call-start
  216.7 43.1 %all-gather.9.cloned.1.call-done = f32[1024,1024]{1,0:T(8,128)} async-done(((f32[64,1024]{1,0:T(8,128)}), f32[1024,1024]{1,0:T(8,128)}) %all-gather.9.cloned.1.call-update) | async-done | bytes 4194320 | tf_op jit(solution)/shard_map/all_gather | solution.py:37
  259.8 17.3 %gather_fusion = f32[1024]{0:T(1024)S(1)} fusion(f32[1024,1024]{1,0:T(8,128)} %all-gather.9.cloned.1.call-done, s32[1024]{0:T(1024)S(1)} %bitcast.19), kind=kCustom, calls=%fused_computation | custom fusion | bytes 16384 | tf_op jit(solution)/shard_map/jit(diagonal)/cond/branch_0_fun/gather | solution.py:39
  277.1 0.6 reduce_sum.18
  278.3 3.9 multiply_reduce_fusion
  282.9 4.9 fusion.9
  287.9 1.9 fusion.22
  289.7 0.0 all-gather.11.cloned.1.call-update
  289.8 0.0 all-gather.13.cloned.1.call-start
  289.8 4.9 fusion.8
  294.7 33.5 %all-gather.11.cloned.1.call-done = bf16[1024,1024]{1,0:T(8,128)(2,1)} async-done(((bf16[64,1024]{1,0:T(8,128)(2,1)}), bf16[1024,1024]{1,0:T(8,128)(2,1)}) %all-gather.11.cloned.1.call-update) | async-done | bytes 2097168 | tf_op jit(solution)/shard_map/all_gather | solution.py:49
  328.2 3.5 fusion.23
  331.7 0.0 all-gather.13.cloned.1.call-update
  331.7 0.2 all-gather.15.cloned.1.call-start
  331.9 0.0 slice-start
  331.9 0.0 slice-start.1
  332.0 4.9 fusion.7
  336.9 33.0 %all-gather.13.cloned.1.call-done = bf16[1024,1024]{1,0:T(8,128)(2,1)} async-done(((bf16[64,1024]{1,0:T(8,128)(2,1)}), bf16[1024,1024]{1,0:T(8,128)(2,1)}) %all-gather.13.cloned.1.call-update) | async-done | bytes 2097168 | tf_op jit(solution)/shard_map/all_gather | solution.py:49
  369.9 3.5 fusion.24
  373.4 0.0 all-gather.15.cloned.1.call-update
  373.4 0.0 all-gather.7.cloned.1.call-start
  373.4 0.1 copy.8
  373.6 0.1 copy.9
  373.7 0.6 compare_select_fusion
  374.3 0.0 all-gather.7.cloned.1.call-update
  374.3 0.0 all-gather.17.cloned.1.call-start
  374.4 4.9 fusion.6
  379.3 32.3 %all-gather.15.cloned.1.call-done = bf16[1024,1024]{1,0:T(8,128)(2,1)} async-done(((bf16[64,1024]{1,0:T(8,128)(2,1)}), bf16[1024,1024]{1,0:T(8,128)(2,1)}) %all-gather.15.cloned.1.call-update) | async-done | bytes 2097168 | tf_op jit(solution)/shard_map/all_gather | solution.py:49
  411.6 3.5 convolution_subtract_fusion.1
  415.1 0.0 all-gather.17.cloned.1.call-update
  415.1 35.2 %all-gather.7.cloned.1.call-done = bf16[512,1024]{0,1:T(8,128)(2,1)} async-done(((bf16[512,64]{0,1:T(8,128)(2,1)}), bf16[512,1024]{0,1:T(8,128)(2,1)}) %all-gather.7.cloned.1.call-update) | async-done | bytes 1048592 | tf_op jit(solution)/shard_map/all_gather | solution.py:58
  450.3 42.8 %all-gather.17.cloned.1.call-done = f32[1024,1024]{1,0:T(8,128)} async-done(((f32[64,1024]{1,0:T(8,128)}), f32[1024,1024]{1,0:T(8,128)}) %all-gather.17.cloned.1.call-update) | async-done | bytes 4194320 | tf_op jit(solution)/shard_map/all_gather | solution.py:54
  493.1 6.1 %fusion.26 = f32[512,1024]{1,0:T(8,128)S(1)} fusion(bf16[512,1024]{0,1:T(8,128)(2,1)} %all-gather.7.cloned.1.call-done, f32[1024,1024]{1,0:T(8,128)} %all-gather.17.cloned.1.call-done), kind=kOutput, calls=%fused_computation.38 | convolution fusion | flops 6442450944 | bytes 7340032 | tf_op jit(solution)/shard_map/dot_general | solution.py:59
  499.2 4.5 fusion.5
  (10 shorter events, 0.0 us)
Async XLA Ops:
  6.5 207.6 %all-reduce.2.cloned.1.call-start = ((), (), s32[]{:S(2)}) async-start(), calls=%async_computation.2 | async-start | bytes 4194304 | tf_op jit(solution)/shard_map/psum | solution.py:35
  8.3 105.9 %copy-start.3 = (bf16[2048,512]{1,0:T(8,128)(2,1)S(1)}, bf16[2048,512]{1,0:T(8,128)(2,1)}, u32[]{:S(2)}) copy-start(bf16[2048,512]{1,0:T(8,128)(2,1)} %param.3) | copy-start | bytes 6291460
  118.0 141.9 %all-gather.9.cloned.1.call-start = ((), (), s32[]{:S(2)}) async-start(), calls=%async_computation.3 | async-start | bytes 4456448 | tf_op jit(solution)/shard_map/all_gather | solution.py:37
  216.6 111.6 %all-gather.11.cloned.1.call-start = ((), (), s32[]{:S(2)}) async-start(), calls=%async_computation.4 | async-start | bytes 2228224 | tf_op jit(solution)/shard_map/all_gather | solution.py:49
  289.8 80.1 %all-gather.13.cloned.1.call-start = ((), (), s32[]{:S(2)}) async-start(), calls=%async_computation.5 | async-start | bytes 2228224 | tf_op jit(solution)/shard_map/all_gather | solution.py:49
  331.7 79.9 %all-gather.15.cloned.1.call-start = ((), (), s32[]{:S(2)}) async-start(), calls=%async_computation.6 | async-start | bytes 2228224 | tf_op jit(solution)/shard_map/all_gather | solution.py:49
  331.9 41.5 %slice-start = ((s32[512,512]{1,0:T(8,128)}), s32[512,64]{1,0:T(8,128)S(1)}, s32[]{:S(2)}) async-start(s32[512,512]{1,0:T(8,128)} %param.5), calls=%async_computation.8 | async-start | bytes 524288 | tf_op jit(solution)/shard_map/slice | solution.py:56
  331.9 41.6 %slice-start.1 = ((bf16[512,512]{1,0:T(8,128)(2,1)}), bf16[512,64]{1,0:T(8,128)(2,1)S(1)}, s32[]{:S(2)}) async-start(bf16[512,512]{1,0:T(8,128)(2,1)} %param.4), calls=%async_computation.9 | async-start | bytes 262144 | tf_op jit(solution)/shard_map/slice | solution.py:56
  373.4 76.9 %all-gather.7.cloned.1.call-start = ((), (), s32[]{:S(2)}) async-start(), calls=%async_computation.1 | async-start | bytes 1114112 | tf_op jit(solution)/shard_map/all_gather | solution.py:58
  374.3 118.8 %all-gather.17.cloned.1.call-start = ((), (), s32[]{:S(2)}) async-start(), calls=%async_computation.7 | async-start | bytes 4456448 | tf_op jit(solution)/shard_map/all_gather | solution.py:54
  415.1 84.1 %copy-start = (f32[512,1024]{1,0:T(8,128)S(1)}, f32[512,1024]{1,0:T(8,128)}, u32[]{:S(2)}) copy-start(f32[512,1024]{1,0:T(8,128)} %all-reduce.2.cloned.1.call-done) | copy-start | bytes 6291460
  415.1 84.1 %copy-start.1 = (s32[512,512]{1,0:T(8,128)S(1)}, s32[512,512]{1,0:T(8,128)}, u32[]{:S(2)}) copy-start(s32[512,512]{1,0:T(8,128)} %param.5) | copy-start | bytes 3145732
  493.1 6.1 %copy-start.2 = (bf16[512,512]{1,0:T(8,128)(2,1)S(1)}, bf16[512,512]{1,0:T(8,128)(2,1)}, u32[]{:S(2)}) copy-start(bf16[512,512]{1,0:T(8,128)(2,1)} %param.4) | copy-start | bytes 1572868
Sparse Core Ops, SparseCore 0:
  118.1 95.9 all-reduce.1
  216.7 43.0 all-gather.8
  289.9 38.2 all-gather.10
  331.8 38.0 all-gather.12
  373.5 38.0 all-gather.14
  413.4 36.8 all-gather.6
  452.3 40.7 all-gather.16
